TPU v7x, 32 devices: a whole 2x2x4 slice. The times are simulated.
32 devices in a mesh: row: 8 (over z, y), col: 4 (over x, core).
Axes of the slice: x: 2, y: 2, z: 4, core: 2. Of those that a mesh axis runs over, the one named last changes fastest.
Arguments:
- leaf_inverse: bfloat16 [32, 1024, 1024], P(('row', 'col')), as said below
- leaf_rhs: bfloat16 [32, 1024, 512], P(('row', 'col')), may hold values from -6 to 6
- leaf_tiles: bfloat16 [32, 1024, 1024], P(('row', 'col')), may hold values from -0.09375 to 0.09375
- mid_inverse_t: bfloat16 [8, 1024, 1024], P('col', None, 'row'), as said below
- mid_rhs: bfloat16 [8, 1024, 512], P('col', 'row'), may hold values from -6 to 6
- mid_tiles: bfloat16 [8, 1024, 1024], P('col', None, 'row'), may hold values from -0.125 to 0.125
- top_inverse_t: bfloat16 [2, 1024, 1024], P(None, None, 'col'), as said below
- top_rhs: bfloat16 [2, 1024, 512], P(None, 'col'), may hold values from -6 to 6
- tile_lists: int32 [32, 1], P(('row', 'col')), may hold values from 0 to 1
Outputs:
- leaf_solved: bfloat16 [32, 1024, 512], P(('row', 'col'))
- mid_solved: bfloat16 [8, 1024, 512], P('col', 'row')
- top_solved: bfloat16 [2, 1024, 512], P(None, 'col')
Inputs may be any that keep to these rules, and one draw needn't show every extreme that they name: Each leaf_inverse[d] is zero above its diagonal and has diagonal entries between 0.75 and 1.25. Each mid_inverse_t[q] is zero below its diagonal and has diagonal entries between 0.75 and 1.25. Each top_inverse_t[b] is zero below its diagonal and has diagonal entries between 0.75 and 1.25.
All inputs are finite; a program needn't handle non-finite values.
Results may differ from a plain program's by a relative error of at most 0.0065.
Values may be sent and summed in bfloat16 or wider, within the bound.
No kernel may reach another device: no remote copies, remote signals or barrier semaphores. Data moves between devices by JAX's collectives and lax.ppermute only.
A program may use at most 64 MiB of HBM per device.

v0:
```python
import jax
import jax.numpy as jnp
from jax import lax
from jax.sharding import PartitionSpec as P

NB = 2


def solve_piece(inverse_cols, piece):
    return lax.dot_general(
        inverse_cols, piece, (((1,), (1,)), ((0,), (0,))), preferred_element_type=jnp.float32
    )


def local(
    leaf_inverse,
    leaf_rhs,
    leaf_tiles,
    mid_inverse_t,
    mid_rhs,
    mid_tiles,
    top_inverse_t,
    top_rhs,
    tile_lists,
):
    slot_ids = jnp.arange(NB, dtype=jnp.int32)[:, None, None]
    solved_leaf = jnp.dot(leaf_inverse[0], leaf_rhs[0], preferred_element_type=jnp.float32).astype(
        jnp.bfloat16
    )
    leaf_update = jnp.dot(leaf_tiles[0], solved_leaf, preferred_element_type=jnp.float32)
    mid_terms = jnp.where(slot_ids == tile_lists[0, 0], leaf_update[None], 0.0)
    mid_share = lax.psum_scatter(mid_terms, "row", scatter_dimension=1, tiled=True)
    mid_resid = (mid_rhs.astype(jnp.float32) - mid_share).astype(jnp.bfloat16)
    mid_own = solve_piece(
        mid_inverse_t, lax.all_gather(mid_resid, "row", axis=1, tiled=True)
    ).astype(jnp.bfloat16)
    top_terms = lax.dot_general(
        mid_tiles, mid_own, (((2,), (1,)), ((0,), (0,))), preferred_element_type=jnp.float32
    )
    summed_rows = lax.psum(top_terms, "row")
    top_share = lax.psum_scatter(summed_rows, "col", scatter_dimension=1, tiled=True)
    top_resid = (top_rhs.astype(jnp.float32) - top_share).astype(jnp.bfloat16)
    top_own = solve_piece(
        top_inverse_t, lax.all_gather(top_resid, "col", axis=1, tiled=True)
    ).astype(jnp.bfloat16)
    return (solved_leaf[None], mid_own, top_own)


def solution(mesh):
    placed = (
        P(("row", "col"), None, None),
        P(("row", "col"), None, None),
        P(("row", "col"), None, None),
        P("col", None, "row"),
        P("col", "row", None),
        P("col", None, "row"),
        P(None, None, "col"),
        P(None, "col", None),
        P(("row", "col"), None),
    )
    return jax.shard_map(
        local,
        mesh=mesh,
        in_specs=placed,
        out_specs=(P(("row", "col"), None, None), P("col", "row", None), P(None, "col", None)),
        check_vma=False,
    )
```

profile of v0, /device:TPU:0, one launch (start us, length us, event | category | flops | bytes accessed | tf_op | source)
XLA Modules:
  0.0 324.7 jit_solution(155862839401762226)
XLA Ops:
  7.2 0.0 copy-start
  7.2 0.0 reduce-scatter.3.cloned.1.call-start
  8.0 0.8 copy-done
  8.8 0.0 copy-start.4
  8.8 2.6 fusion.7
  11.4 0.0 copy-start.5
  11.4 1.0 copy-done.5
  12.4 0.0 copy-done.4
  12.4 1.3 fusion.4
  13.7 2.5 broadcast_select_fusion
  16.2 0.0 copy-start.3
  16.2 0.0 reduce-scatter.3.cloned.1.call-update
  16.2 0.0 all-gather.3.cloned.1.call-start
  16.3 0.9 copy-done.3
  17.2 0.2 copy.12
  17.3 0.0 copy-start.1
  17.4 90.4 %reduce-scatter.3.cloned.1.call-done = f32[2,128,512]{1,2,0:T(8,128)} async-done(((f32[2,1024,512]{1,2,0:T(8,128)}), f32[2,128,512]{1,2,0:T(8,128)}) %reduce-scatter.3.cloned.1.call-update) | async-done | bytes 524304 | tf_op jit(solution)/shard_map/reduce_scatter | solution.py:32
  107.8 1.8 subtract_convert_fusion.1
  109.6 0.0 all-gather.3.cloned.1.call-update
  109.6 0.0 reduce-scatter.5.cloned.1.call-start
  109.7 50.8 %all-gather.3.cloned.1.call-done = bf16[2,1024,512]{1,2,0:T(8,128)(2,1)} async-done(((bf16[2,128,512]{1,2,0:T(8,128)(2,1)}), bf16[2,1024,512]{1,2,0:T(8,128)(2,1)}) %all-gather.3.cloned.1.call-update) | async-done | bytes 2097168 | tf_op jit(solution)/shard_map/all_gather | solution.py:35
  160.4 2.4 convolution_convert_fusion.1
  162.8 0.0 copy-done.1
  162.8 2.7 convolution_bitcast_fusion
  165.5 0.0 copy-start.2
  165.5 0.0 reduce-scatter.5.cloned.1.call-update
  165.5 0.0 all-reduce.2.cloned.1.call-start
  165.5 42.7 %reduce-scatter.5.cloned.1.call-done = f32[2,256,512]{1,2,0:T(8,128)} async-done(((f32[2,1024,512]{1,2,0:T(8,128)}), f32[2,256,512]{1,2,0:T(8,128)}) %reduce-scatter.5.cloned.1.call-update) | async-done | bytes 1048592 | tf_op jit(solution)/shard_map/reduce_scatter | solution.py:41
  208.2 0.0 all-reduce.2.cloned.1.call-update
  208.3 0.0 all-gather.5.cloned.1.call-start
  208.3 0.0 copy-done.2
  208.3 0.2 copy.13
  208.5 81.3 %all-reduce.2.cloned.1.call-done = f32[2,256,512]{1,2,0:T(8,128)} async-done(((f32[2,256,512]{1,2,0:T(8,128)}), f32[2,256,512]{1,2,0:T(8,128)}) %all-reduce.2.cloned.1.call-update) | async-done | bytes 1048592 | tf_op jit(solution)/shard_map/psum | solution.py:40
  289.8 2.1 subtract_convert_fusion
  292.0 0.0 all-gather.5.cloned.1.call-update
  292.0 0.9 copy.14
  292.8 21.7 %all-gather.5.cloned.1.call-done = bf16[2,1024,512]{1,2,0:T(8,128)(2,1)} async-done(((bf16[2,256,512]{1,2,0:T(8,128)(2,1)}), bf16[2,1024,512]{1,2,0:T(8,128)(2,1)}) %all-gather.5.cloned.1.call-update) | async-done | bytes 2097168 | tf_op jit(solution)/shard_map/all_gather | solution.py:44
  314.6 2.6 fusion.10
  317.1 1.0 copy.15
  (1 shorter events, 0.0 us)
Async XLA Ops:
  7.2 1.6 copy-start
  7.2 100.6 %reduce-scatter.3.cloned.1.call-start = ((), (), s32[]{:S(2)}) async-start(), calls=%async_computation.2 | async-start | bytes 4718592 | tf_op jit(solution)/shard_map/reduce_scatter | solution.py:32
  8.8 3.6 %copy-start.4 = (bf16[1,1024,1024]{2,1,0:T(8,128)(2,1)S(1)}, bf16[1,1024,1024]{2,1,0:T(8,128)(2,1)}, u32[]{:S(2)}) copy-start(bf16[1,1024,1024]{2,1,0:T(8,128)(2,1)} %param.11) | copy-start | bytes 6291460
  11.4 1.0 copy-start.5
  16.2 0.9 copy-start.3
  16.2 144.2 %all-gather.3.cloned.1.call-start = ((), (), s32[]{:S(2)}) async-start(), calls=%async_computation.3 | async-start | bytes 2359296 | tf_op jit(solution)/shard_map/all_gather | solution.py:35
  17.3 145.5 %copy-start.1 = (bf16[2,1024,128]{2,1,0:T(8,128)(2,1)S(1)}, bf16[2,1024,128]{2,1,0:T(8,128)(2,1)}, u32[]{:S(2)}) copy-start(bf16[2,1024,128]{2,1,0:T(8,128)(2,1)} %param.14) | copy-start | bytes 1572868
  109.6 98.6 %reduce-scatter.5.cloned.1.call-start = ((), (), s32[]{:S(2)}) async-start(), calls=%async_computation.5 | async-start | bytes 5242880 | tf_op jit(solution)/shard_map/reduce_scatter | solution.py:41
  165.5 42.8 %copy-start.2 = (bf16[2,256,512]{2,1,0:T(8,128)(2,1)S(1)}, bf16[2,256,512]{2,1,0:T(8,128)(2,1)}, u32[]{:S(2)}) copy-start(bf16[2,256,512]{2,1,0:T(8,128)(2,1)} %param.16) | copy-start | bytes 1572868
  165.5 124.3 %all-reduce.2.cloned.1.call-start = ((), (), s32[]{:S(2)}) async-start(), calls=%async_computation.6 | async-start | bytes 2097152 | tf_op jit(solution)/shard_map/psum | solution.py:40
  208.3 106.3 %all-gather.5.cloned.1.call-start = ((), (), s32[]{:S(2)}) async-start(), calls=%async_computation.4 | async-start | bytes 2621440 | tf_op jit(solution)/shard_map/all_gather | solution.py:44
Sparse Core Ops, SparseCore 0:
  16.4 91.3 reduce-scatter.2
  110.4 49.9 all-gather.2
  165.6 42.5 reduce-scatter.4
  211.6 78.1 all-reduce.1
  292.1 22.3 all-gather.4
where the time goes:
time: 325 us
  waiting for transfers between devices  287 us (88%)
  between operations  14.6 us (4%)
  matrix products  11.5 us (4%)
  other arithmetic  6.48 us (2%)
  local copies, waits for them, and re-layouts  4.84 us (1%)
    reduce_scatter x1, waiting for transfers between devices, local(): lax.psum_scatter(mid_terms, 'row', scatter_dimension=1, tiled=True)  90.4 us
    psum x1, waiting for transfers between devices, local(): summed_rows = lax.psum(top_terms, 'row')  81.3 us
    all_gather x1, waiting for transfers between devices, local(): lax.all_gather(mid_resid, 'row', axis=1, tiled=True)  50.8 us
    reduce_scatter x1, waiting for transfers between devices, local(): lax.psum_scatter(summed_rows, 'col', scatter_dimension=1, tiled=True)  42.7 us
    all_gather x1, waiting for transfers between devices, local(): lax.all_gather(top_resid, 'col', axis=1, tiled=True)  21.7 us
  transfers between devices with their start and end apart: 5, of which 5 were waited for; matrix products, arithmetic and copies ran while one was open for 0% of the time, Pallas kernels for 0%

commit v1 on v0

--- a/solution.py
+++ b/solution.py
@@ -37,7 +37,7 @@
     top_terms = lax.dot_general(
         mid_tiles, mid_own, (((2,), (1,)), ((0,), (0,))), preferred_element_type=jnp.float32
     )
-    summed_rows = lax.psum(top_terms, "row")
+    summed_rows = jnp.sum(lax.all_gather(top_terms, "row"), axis=0)
     top_share = lax.psum_scatter(summed_rows, "col", scatter_dimension=1, tiled=True)
     top_resid = (top_rhs.astype(jnp.float32) - top_share).astype(jnp.bfloat16)
     top_own = solve_piece(

time: 325 us -> 908 us (2.79)
  waiting for transfers between devices: 287 us -> 843 us
  other arithmetic: 6.48 us -> 21.7 us
  local copies, waits for them, and re-layouts: 4.84 us -> 16.6 us
    all_gather x0 -> x1, waiting for transfers between devices: none -> 636 us  [local(): summed_rows = jnp.sum(lax.all_gather(top_terms, 'row'), axis=0)]
    psum x1 -> x0, waiting for transfers between devices: 81.3 us -> none  [local(): summed_rows = lax.psum(top_terms, 'row')]
    reduce_sum x0 -> x1, other arithmetic: none -> 15.1 us  [local(): summed_rows = jnp.sum(lax.all_gather(top_terms, 'row'), axis=0)]
where the time goes in v1:
time: 908 us; the launch traced here: 907 us
  waiting for transfers between devices  843 us (93%)
  other arithmetic  21.7 us (2%)
  local copies, waits for them, and re-layouts  16.6 us (2%)
  between operations  14.6 us (2%)
  matrix products  11.4 us (1%)
    all_gather x1, waiting for transfers between devices, local(): summed_rows = jnp.sum(lax.all_gather(top_terms, 'row'), axis=0)  636 us
    reduce_scatter x1, waiting for transfers between devices, local(): lax.psum_scatter(mid_terms, 'row', scatter_dimension=1, tiled=True)  90.5 us
    all_gather x1, waiting for transfers between devices, local(): lax.all_gather(mid_resid, 'row', axis=1, tiled=True)  50.7 us
    reduce_scatter x1, waiting for transfers between devices, local(): lax.psum_scatter(summed_rows, 'col', scatter_dimension=1, tiled=True)  43.3 us
    all_gather x1, waiting for transfers between devices, local(): lax.all_gather(top_resid, 'col', axis=1, tiled=True)  22.1 us
  transfers between devices with their start and end apart: 5, of which 5 were waited for; matrix products, arithmetic and copies ran while one was open for 0% of the time, Pallas kernels for 0%

profile of v1, /device:TPU:0, one launch (start us, length us, event | category | flops | bytes accessed | tf_op | source)
XLA Modules:
  0.0 907.3 jit_solution(14379753893101919449)
XLA Ops:
  7.2 0.0 copy-start
  7.2 0.0 reduce-scatter.3.cloned.1.call-start
  8.0 0.8 copy-done
  8.8 0.0 copy-start.5
  8.8 2.6 fusion.7
  11.4 0.0 copy-start.7
  11.4 1.0 copy-done.7
  12.4 0.0 copy-done.5
  12.4 1.3 fusion.4
  13.7 2.7 broadcast_select_fusion
  16.4 0.0 copy-start.4
  16.4 0.0 copy-start.6
  16.4 0.0 reduce-scatter.3.cloned.1.call-update
  16.4 0.0 all-gather.5.cloned.1.call-start
  16.4 0.9 copy-done.4
  17.3 0.2 copy.21
  17.5 0.0 copy-start.2
  17.5 90.5 %reduce-scatter.3.cloned.1.call-done = f32[2,128,512]{1,2,0:T(8,128)} async-done(((f32[2,1024,512]{1,2,0:T(8,128)}), f32[2,128,512]{1,2,0:T(8,128)}) %reduce-scatter.3.cloned.1.call-update) | async-done | bytes 524304 | tf_op jit(solution)/shard_map/reduce_scatter | solution.py:32
  107.9 1.8 subtract_convert_fusion.1
  109.7 0.0 all-gather.5.cloned.1.call-update
  109.8 0.0 all-gather.9.cloned.1.call-start
  109.8 50.7 %all-gather.5.cloned.1.call-done = bf16[2,1024,512]{1,2,0:T(8,128)(2,1)} async-done(((bf16[2,128,512]{1,2,0:T(8,128)(2,1)}), bf16[2,1024,512]{1,2,0:T(8,128)(2,1)}) %all-gather.5.cloned.1.call-update) | async-done | bytes 2097168 | tf_op jit(solution)/shard_map/all_gather | solution.py:35
  160.6 0.0 copy-done.6
  160.6 2.3 convolution_convert_fusion.1
  162.9 0.0 copy-done.2
  162.9 2.7 convolution_bitcast_fusion
  165.5 5.3 copy.23
  170.9 0.0 all-gather.9.cloned.1.call-update
  170.9 0.0 reduce-scatter.5.cloned.1.call-start
  171.0 636.0 %all-gather.9.cloned.1.call-done = f32[16,1024,512]{2,1,0:T(8,128)} async-done(((f32[2,1024,512]{2,1,0:T(8,128)}), f32[16,1024,512]{2,1,0:T(8,128)}) %all-gather.9.cloned.1.call-update) | async-done | bytes 33554448 | tf_op jit(solution)/shard_map/all_gather | solution.py:40
  806.9 15.1 %reduce_sum.9 = f32[2,1024,512]{2,1,0:T(8,128)} reduce(f32[8,2,1024,512]{3,2,1,0:T(8,128)} %bitcast.31, f32[]{:T(128)} %constant.0.clone.1), dimensions={0}, to_apply=%region_1.2 | reduce | flops 7340032 | bytes 37748740 | tf_op jit(solution)/shard_map/reduce_sum | solution.py:40
  822.0 5.4 copy.24
  827.5 0.0 copy-start.3
  827.5 0.0 reduce-scatter.5.cloned.1.call-update
  827.5 0.0 all-gather.7.cloned.1.call-start
  827.5 1.0 copy-done.3
  828.5 0.2 copy.22
  828.7 43.3 %reduce-scatter.5.cloned.1.call-done = f32[2,256,512]{1,2,0:T(8,128)} async-done(((f32[2,1024,512]{1,2,0:T(8,128)}), f32[2,256,512]{1,2,0:T(8,128)}) %reduce-scatter.5.cloned.1.call-update) | async-done | bytes 1048592 | tf_op jit(solution)/shard_map/reduce_scatter | solution.py:41
  872.0 2.1 subtract_convert_fusion
  874.1 0.0 all-gather.7.cloned.1.call-update
  874.2 0.0 copy-start.1
  874.2 0.9 copy.25
  875.0 22.1 %all-gather.7.cloned.1.call-done = bf16[2,1024,512]{1,2,0:T(8,128)(2,1)} async-done(((bf16[2,256,512]{1,2,0:T(8,128)(2,1)}), bf16[2,1024,512]{1,2,0:T(8,128)(2,1)}) %all-gather.7.cloned.1.call-update) | async-done | bytes 2097168 | tf_op jit(solution)/shard_map/all_gather | solution.py:44
  897.2 2.6 fusion.10
  899.7 1.0 copy.26
  900.7 0.0 copy-done.1
  (1 shorter events, 0.0 us)
Async XLA Ops:
  7.2 1.6 copy-start
  7.2 100.8 %reduce-scatter.3.cloned.1.call-start = ((), (), s32[]{:S(2)}) async-start(), calls=%async_computation.2 | async-start | bytes 4718592 | tf_op jit(solution)/shard_map/reduce_scatter | solution.py:32
  8.8 3.6 copy-start.5
  11.4 1.0 copy-start.7
  16.4 0.9 copy-start.4
  16.4 144.2 %copy-start.6 = (bf16[2,1024,128]{2,1,0:T(8,128)(2,1)S(1)}, bf16[2,1024,128]{2,1,0:T(8,128)(2,1)}, u32[]{:S(2)}) copy-start(bf16[2,1024,128]{2,1,0:T(8,128)(2,1)} %param.12) | copy-start | bytes 1572868
  16.4 144.2 %all-gather.5.cloned.1.call-start = ((), (), s32[]{:S(2)}) async-start(), calls=%async_computation.3 | async-start | bytes 2359296 | tf_op jit(solution)/shard_map/all_gather | solution.py:35
  17.5 145.4 %copy-start.2 = (bf16[2,1024,128]{2,1,0:T(8,128)(2,1)S(1)}, bf16[2,1024,128]{2,1,0:T(8,128)(2,1)}, u32[]{:S(2)}) copy-start(bf16[2,1024,128]{2,1,0:T(8,128)(2,1)} %param.14) | copy-start | bytes 1572868
  109.8 697.1 %all-gather.9.cloned.1.call-start = ((), (), s32[]{:S(2)}) async-start(), calls=%async_computation.6 | async-start | bytes 37748736 | tf_op jit(solution)/shard_map/all_gather | solution.py:40
  170.9 701.1 %reduce-scatter.5.cloned.1.call-start = ((), (), s32[]{:S(2)}) async-start(), calls=%async_computation.4 | async-start | bytes 5242880 | tf_op jit(solution)/shard_map/reduce_scatter | solution.py:41
  827.5 1.0 copy-start.3
  827.5 69.7 %all-gather.7.cloned.1.call-start = ((), (), s32[]{:S(2)}) async-start(), calls=%async_computation.5 | async-start | bytes 2621440 | tf_op jit(solution)/shard_map/all_gather | solution.py:44
  874.2 26.6 %copy-start.1 = (bf16[1,1024,1024]{2,1,0:T(8,128)(2,1)S(1)}, bf16[1,1024,1024]{2,1,0:T(8,128)(2,1)}, u32[]{:S(2)}) copy-start(bf16[1,1024,1024]{2,1,0:T(8,128)(2,1)} %param.9) | copy-start | bytes 6291460
Sparse Core Ops, SparseCore 0:
  16.5 91.3 reduce-scatter.2
  110.6 49.9 all-gather.4
  171.0 635.8 all-gather.8
  827.6 44.3 reduce-scatter.4
  874.3 22.8 all-gather.6
